TPU v7x, 256 devices: a whole 4x4x8 slice. The times are simulated.
256 devices in a mesh: layer: 64 (over y, x_lo, z), feat: 4 (over x_hi, core).
Axes of the slice: x: 4 (x_hi: 2, x_lo: 2; x = x_hi * 2 + x_lo), y: 4, z: 8, core: 2. Of those that a mesh axis runs over, the one named last changes fastest.
Arguments:
- sources: bfloat16 [256, 8192], P(('layer', 'feat')), may hold values from -6 to 6
- targets: bfloat16 [256, 16384], P(('layer', 'feat')), may hold values from -16 to 16
- enc_weight: bfloat16 [8192, 32768], P(None, ('feat', 'layer')), may hold values from -0.0625 to 0.0625
- enc_bias: float32 [32768], P(('feat', 'layer')), may hold values from -3 to 3
- dec_weight: bfloat16 [32768, 16384], P('feat', 'layer'), may hold values from -0.03125 to 0.03125
- dec_bias: float32 [16384], P('layer'), may hold values from -3 to 3
Outputs:
- enc_grad: bfloat16 [8192, 32768], P(None, ('feat', 'layer'))
- dec_grad: bfloat16 [32768, 16384], P('feat', 'layer')
- mse: float32 [], replicated
All inputs are finite; a program needn't handle non-finite values.
Results may differ from a plain program's by a relative error of at most 0.011.
Values may be sent and summed in bfloat16 or wider, within the bound.
No kernel may reach another device: no remote copies, remote signals or barrier semaphores. Data moves between devices by JAX's collectives and lax.ppermute only.
A program may use at most 128 MiB of HBM per device.

v0:
```python
import math
import jax
import jax.numpy as jnp
from jax import lax
from jax.sharding import Mesh, PartitionSpec as P

LAYER = ("y", "x_lo", "z")
FEAT = ("x_hi", "core")


def spread_to(block, axes):
    n = lax.axis_size(axes)
    return lax.all_to_all(
        jnp.broadcast_to(block[None], (n, *block.shape)),
        axes,
        split_axis=0,
        concat_axis=0,
        tiled=True,
    )


def per_device(sources, targets, enc_weight, enc_bias, dec_weight, dec_bias):
    n_y, n_xl, n_z = (lax.axis_size(a) for a in LAYER)
    n_xh, n_c = (lax.axis_size(a) for a in FEAT)
    n_layer = n_y * n_xl * n_z
    rows, width = dec_weight.shape
    feats_own = enc_weight.shape[1]
    depth = sources.shape[1]
    tokens = n_layer * n_xh * n_c
    factor = 1.0 / math.sqrt(tokens)
    owned = lax.all_to_all(
        targets.reshape(n_layer, 1, width), LAYER, split_axis=0, concat_axis=0, tiled=True
    )
    wanted = lax.all_gather(owned.reshape(n_layer, width), FEAT, axis=0, tiled=True)
    wanted = (
        wanted.reshape(n_xh, n_c, n_y * n_xl, n_z, width)
        .transpose(1, 2, 0, 3, 4)
        .reshape(tokens, width)
    )
    near = spread_to(sources, "z").reshape(n_z, depth)
    half = spread_to(near, ("y", "x_lo", "x_hi")).reshape(tokens // n_c, depth)
    inputs = spread_to(half, "core").reshape(tokens, depth)
    preact = jnp.dot(inputs, enc_weight, preferred_element_type=jnp.float32) + enc_bias
    preact = preact.T
    feats = jax.nn.gelu(preact).astype(jnp.bfloat16)
    near_feats = spread_to(feats, "z").reshape(n_z * feats_own, tokens)
    all_feats = spread_to(near_feats, ("y", "x_lo")).reshape(rows, tokens)
    partial_value = lax.dot_general(
        all_feats, dec_weight, (((0,), (0,)), ((), ())), preferred_element_type=jnp.float32
    ).astype(jnp.bfloat16)
    parts = lax.all_gather(partial_value, FEAT, axis=0)
    outputs = jnp.sum(parts.astype(jnp.float32), axis=0) + dec_bias
    misfit = outputs - wanted.astype(jnp.float32)
    errors = (misfit * factor).astype(jnp.bfloat16)
    own_sq = jnp.broadcast_to(jnp.sum(misfit * misfit), (n_layer, 1, 128))
    every_sq = lax.all_to_all(own_sq, LAYER, split_axis=0, concat_axis=0, tiled=True)
    mse = jnp.sum(every_sq[:, 0, 0]) / (tokens * n_layer * width)
    grads = lax.dot_general(
        dec_weight, errors, (((1,), (1,)), ((), ())), preferred_element_type=jnp.float32
    ).astype(jnp.bfloat16)
    far = lax.all_to_all(
        grads.reshape(n_y * n_xl, n_z * feats_own, tokens),
        ("y", "x_lo"),
        split_axis=0,
        concat_axis=0,
        tiled=True,
    )
    far = jnp.sum(far.astype(jnp.float32), axis=0).astype(jnp.bfloat16)
    close = lax.all_to_all(
        far.reshape(n_z, feats_own, tokens), "z", split_axis=0, concat_axis=0, tiled=True
    )
    feat_grad = jnp.sum(close.astype(jnp.float32), axis=0)
    dec_grad = jnp.dot(all_feats, errors, preferred_element_type=jnp.float32).astype(jnp.bfloat16)
    _, pullback = jax.vjp(jax.nn.gelu, preact)
    pre_grad = pullback(feat_grad)[0].astype(jnp.bfloat16)
    enc_grad = lax.dot_general(
        inputs, pre_grad, (((0,), (1,)), ((), ())), preferred_element_type=jnp.float32
    ).astype(jnp.bfloat16)
    return (enc_grad, dec_grad, mse)


def solution(mesh):
    n_layer, n_feat = mesh.devices.shape
    n_x_lo, n_z = (2, 8)
    torus = Mesh(
        mesh.devices.reshape(n_layer // (n_x_lo * n_z), n_x_lo, n_z, n_feat // 2, 2),
        (*LAYER, *FEAT),
    )
    return jax.shard_map(
        per_device,
        mesh=torus,
        in_specs=(
            P((*LAYER, *FEAT), None),
            P((*LAYER, *FEAT), None),
            P(None, (*FEAT, *LAYER)),
            P((*FEAT, *LAYER)),
            P(FEAT, LAYER),
            P(LAYER),
        ),
        out_specs=(P(None, (*FEAT, *LAYER)), P(FEAT, LAYER), P()),
        check_vma=False,
    )
```

profile of v0, /device:TPU:1, one launch (start us, length us, event | category | flops | bytes accessed | tf_op | source)
XLA Modules:
  0.0 274.8 jit_solution(3152163767902077613)
XLA Ops:
  0.6 0.0 copy-start
  0.6 1.0 reduce.3
  1.6 0.0 copy-start.2
  1.7 0.1 broadcast_in_dim.41
  1.8 0.5 broadcast.54
  2.3 1.4 reduce.4
  3.7 0.1 reshape.69
  3.8 16.6 %all_to_all.45 = bf16[8,2,4096]{2,1,0:T(2,128)(2,1)S(1)} all-to-all(bf16[8,2,4096]{2,1,0:T(2,128)(2,1)S(1)} %reshape.69), channel_id=1, replica_groups=mesh['y'=4,'x_lo'=2,'z'=8,'x_hi'=2,'core'=2] {'z'}, dimensions={0} | all-to-all | bytes 262144 | tf_op jit(solution)/shard_map/all_to_all | solution.py:13
  20.4 0.1 reshape.70
  20.5 0.2 copy.73
  20.6 1.5 broadcast_in_dim.43
  22.2 6.8 %all-to-all-start.1 = ((bf16[16,8,8192]{2,1,0:T(8,128)(2,1)}), bf16[16,8,8192]{2,1,0:T(8,128)(2,1)}, u32[]{:S(2)}, u32[]{:S(2)}) async-start(bf16[16,8,8192]{2,1,0:T(8,128)(2,1)} %broadcast_in_dim.43), calls=%async_computation.1 | async-start | bytes 4194304 | tf_op jit(solution)/shard_map/all_to_all | solution.py:13
  29.0 0.8 reduce.5
  29.8 0.6 reshape.71
  30.5 23.9 %all-to-all-done.1 = bf16[16,8,8192]{2,1,0:T(8,128)(2,1)} async-done(((bf16[16,8,8192]{2,1,0:T(8,128)(2,1)}), bf16[16,8,8192]{2,1,0:T(8,128)(2,1)}, u32[]{:S(2)}, u32[]{:S(2)}) %all-to-all-start.1) | async-done | bytes 2097184 | tf_op jit(solution)/shard_map/all_to_all | solution.py:13
  54.3 2.1 broadcast_in_dim.45
  56.4 0.0 copy-start.4
  56.4 10.4 %all_to_all.46 = bf16[2,128,8192]{2,1,0:T(8,128)(2,1)} all-to-all(bf16[2,128,8192]{2,1,0:T(8,128)(2,1)S(1)} %broadcast_in_dim.45), channel_id=1, replica_groups=mesh['y'=4,'x_lo'=2,'z'=8,'x_hi'=2,'core'=2] {'core'}, dimensions={0} | all-to-all | bytes 8388608 | tf_op jit(solution)/shard_map/all_to_all | solution.py:13
  66.8 5.7 %all-to-all-start.5 = ((bf16[64,2,128]{2,1,0:T(2,128)(2,1)}), bf16[64,2,128]{2,1,0:T(2,128)(2,1)S(1)}, u32[]{:S(2)}, u32[]{:S(2)}) async-start(bf16[64,2,128]{2,1,0:T(2,128)(2,1)} %reshape.71), calls=%async_computation.5 | async-start | bytes 65536 | tf_op jit(solution)/shard_map/all_to_all | solution.py:31
  72.6 3.7 %multiply_convert_fusion.1 = (bf16[128,256]{1,0:T(8,128)(2,1)S(1)}, f32[128,256]{1,0:T(8,128)S(1)}) fusion(f32[128]{0:T(128)S(1)} %copy-done.4, bf16[8192,128]{1,0:T(8,128)(2,1)S(1)} %copy-done, bf16[256,8192]{1,0:T(8,128)(2,1)} %bitcast.47), kind=kOutput, calls=%fused_computation.28 | convolution fusion | flops 537198592 | bytes 6488576 | tf_op jit(solution)/shard_map/dot_general | solution.py:43
  76.3 5.5 %all-to-all-done.5 = bf16[64,2,128]{2,1,0:T(2,128)(2,1)S(1)} async-done(((bf16[64,2,128]{2,1,0:T(2,128)(2,1)}), bf16[64,2,128]{2,1,0:T(2,128)(2,1)S(1)}, u32[]{:S(2)}, u32[]{:S(2)}) %all-to-all-start.5) | async-done | bytes 32800 | tf_op jit(solution)/shard_map/all_to_all | solution.py:31
  81.8 17.4 %all_to_all.47 = bf16[8,128,256]{2,1,0:T(8,128)(2,1)S(1)} all-to-all(bf16[8,128,256]{2,1,0:T(8,128)(2,1)S(1)} %broadcast_in_dim.46), channel_id=1, replica_groups=mesh['y'=4,'x_lo'=2,'z'=8,'x_hi'=2,'core'=2] {'z'}, dimensions={0} | all-to-all | bytes 1048576 | tf_op jit(solution)/shard_map/all_to_all | solution.py:13
  99.3 2.3 broadcast_in_dim.48
  101.6 4.5 %all-to-all-start.4 = ((bf16[8,1024,256]{2,1,0:T(8,128)(2,1)}), bf16[8,1024,256]{2,1,0:T(8,128)(2,1)}, u32[]{:S(2)}, u32[]{:S(2)}) async-start(bf16[8,1024,256]{2,1,0:T(8,128)(2,1)} %broadcast_in_dim.48), calls=%async_computation.4 | async-start | bytes 8388608 | tf_op jit(solution)/shard_map/all_to_all | solution.py:13
  106.2 51.4 %all-gather.1 = bf16[256,1,256]{2,0,1:T(8,128)(2,1)S(1)} all-gather(bf16[64,1,256]{2,0,1:T(8,128)(2,1)S(1)} %copy.44), channel_id=3, replica_groups=mesh['y'=4,'x_lo'=2,'z'=8,'x_hi'=2,'core'=2] {'x_hi','core'}, dimensions={0}, use_global_device_ids=true | all-gather | bytes 163840 | tf_op jit(solution)/shard_map/all_gather | solution.py:34
  157.6 0.0 copy-start.3
  157.7 0.0 copy-start.1
  157.7 4.9 %convolution_convert_fusion.3 = bf16[256,256]{1,0:T(8,128)(2,1)S(1)} fusion(bf16[8192,256]{1,0:T(8,128)(2,1)} %bitcast.3, bf16[8192,256]{1,0:T(8,128)(2,1)} %param.10), kind=kOutput, calls=%fused_computation.5 | convolution fusion | flops 1073807360 | bytes 8519680 | tf_op jit(solution)/shard_map/dot_general | solution.py:48
  162.6 8.8 %all-gather = bf16[1024,256]{1,0:T(8,128)(2,1)S(1)} all-gather(bf16[256,256]{1,0:T(8,128)(2,1)S(1)} %convolution_convert_fusion.3), channel_id=2, replica_groups=mesh['y'=4,'x_lo'=2,'z'=8,'x_hi'=2,'core'=2] {'x_hi','core'}, dimensions={0}, use_global_device_ids=true | all-gather | bytes 655360 | tf_op jit(solution)/shard_map/all_gather | solution.py:51
  171.4 0.1 convert_reduce_fusion
  171.5 1.3 convolution_convert_fusion.1
  172.8 2.5 copy.72
  175.2 4.9 %all-to-all-start.6 = ((bf16[8,1024,256]{1,2,0:T(8,128)(2,1)}), bf16[8,1024,256]{1,2,0:T(8,128)(2,1)}, u32[]{:S(2)}, u32[]{:S(2)}) async-start(bf16[8,1024,256]{1,2,0:T(8,128)(2,1)} %bitcast.49), calls=%async_computation.6 | async-start | bytes 8388608 | tf_op jit(solution)/shard_map/all_to_all | solution.py:61
  180.2 0.7 multiply_reduce_fusion
  180.8 48.5 %all-to-all-done.6 = bf16[8,1024,256]{1,2,0:T(8,128)(2,1)} async-done(((bf16[8,1024,256]{1,2,0:T(8,128)(2,1)}), bf16[8,1024,256]{1,2,0:T(8,128)(2,1)}, u32[]{:S(2)}, u32[]{:S(2)}) %all-to-all-start.6) | async-done | bytes 4194336 | tf_op jit(solution)/shard_map/all_to_all | solution.py:61
  229.4 1.3 broadcast_in_dim.49
  230.7 5.8 %all-to-all-start.8 = ((f32[64,1,128]{2,1,0:T(1,128)}), f32[64,1,128]{2,1,0:T(1,128)S(1)}, u32[]{:S(2)}, u32[]{:S(2)}) async-start(f32[64,1,128]{2,1,0:T(1,128)} %broadcast_in_dim.49), calls=%async_computation.8 | async-start | bytes 65536 | tf_op jit(solution)/shard_map/all_to_all | solution.py:56
  236.5 3.1 %reduce_sum.51 = bf16[1024,256]{0,1:T(8,128)(2,1)S(1)} reduce(bf16[8,1024,256]{1,2,0:T(8,128)(2,1)} %all-to-all-done.6, bf16[]{:T(256)} %constant.17.clone.1), dimensions={0}, to_apply=%region_1.0 | reduce | flops 1835008 | bytes 4718594 | tf_op jit(solution)/shard_map/reduce_sum | solution.py:68
  239.6 0.9 copy_bitcast_fusion.1
  240.5 5.2 %all-to-all-done.8 = f32[64,1,128]{2,1,0:T(1,128)S(1)} async-done(((f32[64,1,128]{2,1,0:T(1,128)}), f32[64,1,128]{2,1,0:T(1,128)S(1)}, u32[]{:S(2)}, u32[]{:S(2)}) %all-to-all-start.8) | async-done | bytes 32800 | tf_op jit(solution)/shard_map/all_to_all | solution.py:56
  245.7 3.7 %all-to-all-start.7 = ((bf16[8,128,256]{1,2,0:T(8,128)(2,1)}), bf16[8,128,256]{1,2,0:T(8,128)(2,1)S(1)}, u32[]{:S(2)}, u32[]{:S(2)}) async-start(bf16[8,128,256]{1,2,0:T(8,128)(2,1)} %copy_bitcast_fusion.1), calls=%async_computation.7 | async-start | bytes 1048576 | tf_op jit(solution)/shard_map/all_to_all | solution.py:69
  249.4 5.5 %convolution_convert_fusion = bf16[8192,256]{1,0:T(8,128)(2,1)} fusion(bf16[8192,256]{1,0:T(8,128)(2,1)} %bitcast.3, bf16[256,256]{1,0:T(8,128)(2,1)S(1)} %bitcast.56), kind=kOutput, calls=%fused_computation | convolution fusion | flops 1075838976 | bytes 8519680 | tf_op jit(solution)/shard_map/dot_general | solution.py:73
  254.9 0.7 slice_reduce_fusion
  256.2 9.0 %all-to-all-done.7 = bf16[8,128,256]{1,2,0:T(8,128)(2,1)S(1)} async-done(((bf16[8,128,256]{1,2,0:T(8,128)(2,1)}), bf16[8,128,256]{1,2,0:T(8,128)(2,1)S(1)}, u32[]{:S(2)}, u32[]{:S(2)}) %all-to-all-start.7) | async-done | bytes 524320 | tf_op jit(solution)/shard_map/all_to_all | solution.py:69
  265.1 0.1 convert_reduce_fusion.1
  265.2 0.1 copy.50
  265.3 4.3 %fusion = bf16[8192,128]{0,1:T(8,128)(2,1)} fusion(bf16[256,8192]{1,0:T(8,128)(2,1)} %bitcast.48, f32[128,256]{1,0:T(8,128)S(1)} %get-tuple-element.27, f32[128,256]{1,0:T(8,128)S(1)} %copy.50), kind=kOutput, calls=%fused_computation.3 | convolution fusion | flops 538574848 | bytes 6553600 | tf_op jit(solution)/shard_map/dot_general | solution.py:76
  269.6 4.1 %copy.55 = bf16[8192,128]{1,0:T(8,128)(2,1)} copy(bf16[8192,128]{0,1:T(8,128)(2,1)} %fusion) | data formatting | bytes 4194304
  (13 shorter events, 0.2 us)
Async XLA Ops:
  0.6 71.9 %copy-start = (bf16[8192,128]{1,0:T(8,128)(2,1)S(1)}, bf16[8192,128]{1,0:T(8,128)(2,1)}, u32[]{:S(2)}) copy-start(bf16[8192,128]{1,0:T(8,128)(2,1)} %param.8) | copy-start | bytes 6291460
  1.6 27.3 %copy-start.2 = (bf16[1,16384]{1,0:T(2,128)(2,1)S(1)}, bf16[1,16384]{1,0:T(2,128)(2,1)}, u32[]{:S(2)}) copy-start(bf16[1,16384]{1,0:T(2,128)(2,1)} %param.7) | copy-start | bytes 98308
  22.2 32.2 %all-to-all-start.1 = ((bf16[16,8,8192]{2,1,0:T(8,128)(2,1)}), bf16[16,8,8192]{2,1,0:T(8,128)(2,1)}, u32[]{:S(2)}, u32[]{:S(2)}) async-start(bf16[16,8,8192]{2,1,0:T(8,128)(2,1)} %broadcast_in_dim.43), calls=%async_computation.1 | async-start | bytes 4194304 | tf_op jit(solution)/shard_map/all_to_all | solution.py:13
  56.4 16.2 %copy-start.4 = (f32[128]{0:T(128)S(1)}, f32[128]{0:T(128)}, u32[]{:S(2)}) copy-start(f32[128]{0:T(128)} %param.9) | copy-start | bytes 1540
  66.8 15.0 %all-to-all-start.5 = ((bf16[64,2,128]{2,1,0:T(2,128)(2,1)}), bf16[64,2,128]{2,1,0:T(2,128)(2,1)S(1)}, u32[]{:S(2)}, u32[]{:S(2)}) async-start(bf16[64,2,128]{2,1,0:T(2,128)(2,1)} %reshape.71), calls=%async_computation.5 | async-start | bytes 65536 | tf_op jit(solution)/shard_map/all_to_all | solution.py:31
  101.6 56.1 %all-to-all-start.4 = ((bf16[8,1024,256]{2,1,0:T(8,128)(2,1)}), bf16[8,1024,256]{2,1,0:T(8,128)(2,1)}, u32[]{:S(2)}, u32[]{:S(2)}) async-start(bf16[8,1024,256]{2,1,0:T(8,128)(2,1)} %broadcast_in_dim.48), calls=%async_computation.4 | async-start | bytes 8388608 | tf_op jit(solution)/shard_map/all_to_all | solution.py:13
  157.6 13.8 %copy-start.3 = (f32[256]{0:T(256)S(1)}, f32[256]{0:T(256)}, u32[]{:S(2)}) copy-start(f32[256]{0:T(256)} %param.11) | copy-start | bytes 3076
  157.7 13.8 %copy-start.1 = (bf16[8192,256]{1,0:T(8,128)(2,1)S(1)}, bf16[8192,256]{1,0:T(8,128)(2,1)}, u32[]{:S(2)}) copy-start(bf16[8192,256]{1,0:T(8,128)(2,1)} %param.10) | copy-start | bytes 12582916
  175.2 54.1 %all-to-all-start.6 = ((bf16[8,1024,256]{1,2,0:T(8,128)(2,1)}), bf16[8,1024,256]{1,2,0:T(8,128)(2,1)}, u32[]{:S(2)}, u32[]{:S(2)}) async-start(bf16[8,1024,256]{1,2,0:T(8,128)(2,1)} %bitcast.49), calls=%async_computation.6 | async-start | bytes 8388608 | tf_op jit(solution)/shard_map/all_to_all | solution.py:61
  230.7 15.0 %all-to-all-start.8 = ((f32[64,1,128]{2,1,0:T(1,128)}), f32[64,1,128]{2,1,0:T(1,128)S(1)}, u32[]{:S(2)}, u32[]{:S(2)}) async-start(f32[64,1,128]{2,1,0:T(1,128)} %broadcast_in_dim.49), calls=%async_computation.8 | async-start | bytes 65536 | tf_op jit(solution)/shard_map/all_to_all | solution.py:56
  245.7 19.4 %all-to-all-start.7 = ((bf16[8,128,256]{1,2,0:T(8,128)(2,1)}), bf16[8,128,256]{1,2,0:T(8,128)(2,1)S(1)}, u32[]{:S(2)}, u32[]{:S(2)}) async-start(bf16[8,128,256]{1,2,0:T(8,128)(2,1)} %copy_bitcast_fusion.1), calls=%async_computation.7 | async-start | bytes 1048576 | tf_op jit(solution)/shard_map/all_to_all | solution.py:69
where the time goes:
time: 276 us; the launch traced here: 275 us
  blocking collectives  105 us (38%)
  waiting for transfers between devices  92.1 us (33%)
  starting transfers between devices  31.5 us (11%)
  matrix products  19.7 us (7%)
  local copies, waits for them, and re-layouts  16.4 us (6%)
  other arithmetic  7.86 us (3%)
    all_gather x1, blocking collectives, per_device(): lax.all_gather(owned.reshape(n_layer, width), FEAT, axis=0, tiled=True)  51.4 us
    all_to_all x1, waiting for transfers between devices, per_device(): lax.all_to_all(grads.reshape(n_y * n_xl, n_z * feats_own, tokens), ('y',...  48.5 us
    all_to_all x3, blocking collectives, spread_to(): lax.all_to_all(jnp.broadcast_to(block[None], (n, *block.shape)), axes, sp...  44.4 us
    all_to_all x2, waiting for transfers between devices, spread_to(): lax.all_to_all(jnp.broadcast_to(block[None], (n, *block.shape)), axes, sp...  23.9 us
    all_to_all x2, starting transfers between devices, spread_to(): lax.all_to_all(jnp.broadcast_to(block[None], (n, *block.shape)), axes, sp...  11.4 us
    all_to_all x1, waiting for transfers between devices, per_device(): lax.all_to_all(far.reshape(n_z, feats_own, tokens), 'z', split_axis=0, co...  8.96 us
    all_gather x1, blocking collectives, per_device(): parts = lax.all_gather(partial_value, FEAT, axis=0)  8.78 us
    broadcast_in_dim x6, local copies, waits for them, and re-layouts, spread_to(): jnp.broadcast_to(block[None], (n, *block.shape))  6.54 us
  transfers between devices with their start and end apart: 6, of which 5 were waited for; matrix products, arithmetic and copies ran while one was open for 6% of the time, Pallas kernels for 0%

commit v1 on v0

--- a/solution.py
+++ b/solution.py
@@ -31,7 +31,12 @@
     owned = lax.all_to_all(
         targets.reshape(n_layer, 1, width), LAYER, split_axis=0, concat_axis=0, tiled=True
     )
-    wanted = lax.all_gather(owned.reshape(n_layer, width), FEAT, axis=0, tiled=True)
+    wanted = jnp.concatenate(
+        lax.all_to_all(
+            jnp.stack([owned.reshape(n_layer, width)] * lax.axis_size(FEAT)), FEAT, 0, 0
+        ),
+        axis=0,
+    )
     wanted = (
         wanted.reshape(n_xh, n_c, n_y * n_xl, n_z, width)
         .transpose(1, 2, 0, 3, 4)

time: 276 us -> 285 us (1.033)
  blocking collectives: 105 us -> 42.8 us
  waiting for transfers between devices: 92.1 us -> 149 us
  starting transfers between devices: 31.5 us -> 43.4 us
    all_to_all x2 -> x3, waiting for transfers between devices: 23.9 us -> 76.5 us  [spread_to(): lax.all_to_all(jnp.broadcast_to(block[None], (n, *block.shape)), axes, sp...]
    all_gather x1 -> x0, blocking collectives: 51.4 us -> none  [per_device(): lax.all_gather(owned.reshape(n_layer, width), FEAT, axis=0, tiled=True)]
    all_to_all x3 -> x2, blocking collectives: 44.4 us -> 30.1 us  [spread_to(): lax.all_to_all(jnp.broadcast_to(block[None], (n, *block.shape)), axes, sp...]
    all_to_all x2 -> x3, starting transfers between devices: 11.4 us -> 18.1 us  [spread_to(): lax.all_to_all(jnp.broadcast_to(block[None], (n, *block.shape)), axes, sp...]
    all_to_all x0 -> x1, starting transfers between devices: none -> 5.53 us  [per_device(): lax.all_to_all(jnp.stack([owned.reshape(n_layer, width)] * lax.axis_size(...]
    all_gather x1, blocking collectives: 8.78 us -> 12.7 us  [per_device(): parts = lax.all_gather(partial_value, FEAT, axis=0)]
    all_to_all x1, waiting for transfers between devices: 5.48 us -> 8.92 us  [per_device(): lax.all_to_all(targets.reshape(n_layer, 1, width), LAYER, split_axis=0, c...]
    unnamed x16 -> x15, local copies, waits for them, and re-layouts: 5.09 us -> 5.75 us
  transfers between devices with their start and end apart: 6 -> 8, of which waited for: 5 -> 8; matrix products, arithmetic and copies ran while one was open for 6% -> 6% of each run, Pallas kernels for 0% -> 0%
where the time goes in v1:
time: 285 us; the launch traced here: 284 us
  waiting for transfers between devices  149 us (52%)
  starting transfers between devices  43.4 us (15%)
  blocking collectives  42.8 us (15%)
  matrix products  19.7 us (7%)
  local copies, waits for them, and re-layouts  17.7 us (6%)
  other arithmetic  8.7 us (3%)
    all_to_all x3, waiting for transfers between devices, spread_to(): lax.all_to_all(jnp.broadcast_to(block[None], (n, *block.shape)), axes, sp...  76.5 us
    all_to_all x1, waiting for transfers between devices, per_device(): lax.all_to_all(grads.reshape(n_y * n_xl, n_z * feats_own, tokens), ('y',...  48.7 us
    all_to_all x2, blocking collectives, spread_to(): lax.all_to_all(jnp.broadcast_to(block[None], (n, *block.shape)), axes, sp...  30.1 us
    all_to_all x3, starting transfers between devices, spread_to(): lax.all_to_all(jnp.broadcast_to(block[None], (n, *block.shape)), axes, sp...  18.1 us
    all_gather x1, blocking collectives, per_device(): parts = lax.all_gather(partial_value, FEAT, axis=0)  12.7 us
    all_to_all x1, waiting for transfers between devices, per_device(): lax.all_to_all(targets.reshape(n_layer, 1, width), LAYER, split_axis=0, c...  8.92 us
    all_to_all x1, waiting for transfers between devices, per_device(): lax.all_to_all(far.reshape(n_z, feats_own, tokens), 'z', split_axis=0, co...  8.67 us
    all_to_all x1, starting transfers between devices, per_device(): lax.all_to_all(targets.reshape(n_layer, 1, width), LAYER, split_axis=0, c...  6.85 us
  transfers between devices with their start and end apart: 8, of which 8 were waited for; matrix products, arithmetic and copies ran while one was open for 6% of the time, Pallas kernels for 0%

profile of v1, /device:TPU:1, one launch (start us, length us, event | category | flops | bytes accessed | tf_op | source)
XLA Modules:
  0.0 284.2 jit_solution(16637828269328250067)
XLA Ops:
  0.6 0.0 copy-start
  0.6 1.0 reduce.3
  1.6 0.1 broadcast_in_dim.41
  1.8 0.5 broadcast.55
  2.3 1.4 reduce.4
  3.7 0.7 reshape.61
  4.4 9.0 %all-to-all-start = ((bf16[8,2,4096]{2,1,0:T(2,128)(2,1)}), bf16[8,2,4096]{2,1,0:T(2,128)(2,1)S(1)}, u32[]{:S(2)}, u32[]{:S(2)}) async-start(bf16[8,2,4096]{2,1,0:T(2,128)(2,1)} %reshape.61), calls=%async_computation | async-start | bytes 262144 | tf_op jit(solution)/shard_map/all_to_all | solution.py:13
  13.5 1.7 reduce.5
  15.1 0.6 reshape.63
  15.7 5.5 %all-to-all-done = bf16[8,2,4096]{2,1,0:T(2,128)(2,1)S(1)} async-done(((bf16[8,2,4096]{2,1,0:T(2,128)(2,1)}), bf16[8,2,4096]{2,1,0:T(2,128)(2,1)S(1)}, u32[]{:S(2)}, u32[]{:S(2)}) %all-to-all-start) | async-done | bytes 131104 | tf_op jit(solution)/shard_map/all_to_all | solution.py:13
  21.2 6.9 %all-to-all-start.5 = ((bf16[64,2,128]{2,1,0:T(2,128)(2,1)}), bf16[64,2,128]{2,1,0:T(2,128)(2,1)S(1)}, u32[]{:S(2)}, u32[]{:S(2)}) async-start(bf16[64,2,128]{2,1,0:T(2,128)(2,1)} %reshape.63), calls=%async_computation.5 | async-start | bytes 65536 | tf_op jit(solution)/shard_map/all_to_all | solution.py:31
  28.1 0.1 reshape.62
  28.2 0.2 copy.77
  28.4 8.9 %all-to-all-done.5 = bf16[64,2,128]{2,1,0:T(2,128)(2,1)S(1)} async-done(((bf16[64,2,128]{2,1,0:T(2,128)(2,1)}), bf16[64,2,128]{2,1,0:T(2,128)(2,1)S(1)}, u32[]{:S(2)}, u32[]{:S(2)}) %all-to-all-start.5) | async-done | bytes 32800 | tf_op jit(solution)/shard_map/all_to_all | solution.py:31
  37.3 1.5 broadcast_in_dim.43
  38.8 4.6 %all-to-all-start.1 = ((bf16[16,8,8192]{2,1,0:T(8,128)(2,1)}), bf16[16,8,8192]{2,1,0:T(8,128)(2,1)}, u32[]{:S(2)}, u32[]{:S(2)}) async-start(bf16[16,8,8192]{2,1,0:T(8,128)(2,1)} %broadcast_in_dim.43), calls=%async_computation.1 | async-start | bytes 4194304 | tf_op jit(solution)/shard_map/all_to_all | solution.py:13
  43.4 24.0 %all-to-all-done.1 = bf16[16,8,8192]{2,1,0:T(8,128)(2,1)} async-done(((bf16[16,8,8192]{2,1,0:T(8,128)(2,1)}), bf16[16,8,8192]{2,1,0:T(8,128)(2,1)}, u32[]{:S(2)}, u32[]{:S(2)}) %all-to-all-start.1) | async-done | bytes 2097184 | tf_op jit(solution)/shard_map/all_to_all | solution.py:13
  67.4 2.1 broadcast_in_dim.45
  69.5 11.7 %all_to_all.50 = bf16[2,128,8192]{2,1,0:T(8,128)(2,1)} all-to-all(bf16[2,128,8192]{2,1,0:T(8,128)(2,1)S(1)} %broadcast_in_dim.45), channel_id=1, replica_groups=mesh['y'=4,'x_lo'=2,'z'=8,'x_hi'=2,'core'=2] {'core'}, dimensions={0} | all-to-all | bytes 8388608 | tf_op jit(solution)/shard_map/all_to_all | solution.py:13
  81.2 0.7 stack.3
  81.9 5.5 %all-to-all-start.6 = ((bf16[4,64,256]{2,1,0:T(8,128)(2,1)}), bf16[4,64,256]{2,1,0:T(8,128)(2,1)S(1)}, u32[]{:S(2)}, u32[]{:S(2)}) async-start(bf16[4,64,256]{2,1,0:T(8,128)(2,1)} %stack.3), calls=%async_computation.6 | async-start | bytes 262144 | tf_op jit(solution)/shard_map/all_to_all | solution.py:35
  87.4 3.7 %multiply_convert_fusion.1 = (bf16[128,256]{1,0:T(8,128)(2,1)S(1)}, f32[128,256]{1,0:T(8,128)S(1)}) fusion(f32[128]{0:T(128)S(1)} %copy-done.3, bf16[8192,128]{1,0:T(8,128)(2,1)S(1)} %copy-done, bf16[256,8192]{1,0:T(8,128)(2,1)} %bitcast.50), kind=kOutput, calls=%fused_computation.28 | convolution fusion | flops 537198592 | bytes 6488576 | tf_op jit(solution)/shard_map/dot_general | solution.py:48
  91.2 1.3 all-to-all-done.6
  92.5 18.3 %all_to_all.51 = bf16[8,128,256]{2,1,0:T(8,128)(2,1)S(1)} all-to-all(bf16[8,128,256]{2,1,0:T(8,128)(2,1)S(1)} %broadcast_in_dim.46), channel_id=1, replica_groups=mesh['y'=4,'x_lo'=2,'z'=8,'x_hi'=2,'core'=2] {'z'}, dimensions={0} | all-to-all | bytes 1048576 | tf_op jit(solution)/shard_map/all_to_all | solution.py:13
  110.9 2.3 broadcast_in_dim.48
  113.2 4.5 %all-to-all-start.4 = ((bf16[8,1024,256]{2,1,0:T(8,128)(2,1)}), bf16[8,1024,256]{2,1,0:T(8,128)(2,1)}, u32[]{:S(2)}, u32[]{:S(2)}) async-start(bf16[8,1024,256]{2,1,0:T(8,128)(2,1)} %broadcast_in_dim.48), calls=%async_computation.4 | async-start | bytes 8388608 | tf_op jit(solution)/shard_map/all_to_all | solution.py:13
  117.8 47.0 %all-to-all-done.4 = bf16[8,1024,256]{2,1,0:T(8,128)(2,1)} async-done(((bf16[8,1024,256]{2,1,0:T(8,128)(2,1)}), bf16[8,1024,256]{2,1,0:T(8,128)(2,1)}, u32[]{:S(2)}, u32[]{:S(2)}) %all-to-all-start.4) | async-done | bytes 4194336 | tf_op jit(solution)/shard_map/all_to_all | solution.py:13
  164.8 4.9 %convolution_convert_fusion.3 = bf16[256,256]{1,0:T(8,128)(2,1)S(1)} fusion(bf16[8192,256]{1,0:T(8,128)(2,1)} %bitcast.3, bf16[8192,256]{1,0:T(8,128)(2,1)} %param.10), kind=kOutput, calls=%fused_computation.5 | convolution fusion | flops 1073807360 | bytes 8519680 | tf_op jit(solution)/shard_map/dot_general | solution.py:53
  169.7 12.7 %all-gather = bf16[1024,256]{1,0:T(8,128)(2,1)S(1)} all-gather(bf16[256,256]{1,0:T(8,128)(2,1)S(1)} %convolution_convert_fusion.3), channel_id=2, replica_groups=mesh['y'=4,'x_lo'=2,'z'=8,'x_hi'=2,'core'=2] {'x_hi','core'}, dimensions={0}, use_global_device_ids=true | all-gather | bytes 655360 | tf_op jit(solution)/shard_map/all_gather | solution.py:56
  182.4 0.1 convert_reduce_fusion
  182.5 1.3 convolution_convert_fusion.1
  183.8 2.5 copy.76
  186.3 4.6 %all-to-all-start.7 = ((bf16[8,1024,256]{1,2,0:T(8,128)(2,1)}), bf16[8,1024,256]{1,2,0:T(8,128)(2,1)}, u32[]{:S(2)}, u32[]{:S(2)}) async-start(bf16[8,1024,256]{1,2,0:T(8,128)(2,1)} %bitcast.52), calls=%async_computation.7 | async-start | bytes 8388608 | tf_op jit(solution)/shard_map/all_to_all | solution.py:66
  190.9 0.7 multiply_reduce_fusion
  191.5 48.7 %all-to-all-done.7 = bf16[8,1024,256]{1,2,0:T(8,128)(2,1)} async-done(((bf16[8,1024,256]{1,2,0:T(8,128)(2,1)}), bf16[8,1024,256]{1,2,0:T(8,128)(2,1)}, u32[]{:S(2)}, u32[]{:S(2)}) %all-to-all-start.7) | async-done | bytes 4194336 | tf_op jit(solution)/shard_map/all_to_all | solution.py:66
  240.3 1.3 broadcast_in_dim.49
  241.6 4.6 %all-to-all-start.9 = ((f32[64,1,128]{2,1,0:T(1,128)}), f32[64,1,128]{2,1,0:T(1,128)S(1)}, u32[]{:S(2)}, u32[]{:S(2)}) async-start(f32[64,1,128]{2,1,0:T(1,128)} %broadcast_in_dim.49), calls=%async_computation.9 | async-start | bytes 65536 | tf_op jit(solution)/shard_map/all_to_all | solution.py:61
  246.2 3.1 %reduce_sum.51 = bf16[1024,256]{0,1:T(8,128)(2,1)S(1)} reduce(bf16[8,1024,256]{1,2,0:T(8,128)(2,1)} %all-to-all-done.7, bf16[]{:T(256)} %constant.17.clone.1), dimensions={0}, to_apply=%region_1.0 | reduce | flops 1835008 | bytes 4718594 | tf_op jit(solution)/shard_map/reduce_sum | solution.py:73
  249.3 0.9 copy_bitcast_fusion.1
  250.1 5.2 %all-to-all-done.9 = f32[64,1,128]{2,1,0:T(1,128)S(1)} async-done(((f32[64,1,128]{2,1,0:T(1,128)}), f32[64,1,128]{2,1,0:T(1,128)S(1)}, u32[]{:S(2)}, u32[]{:S(2)}) %all-to-all-start.9) | async-done | bytes 32800 | tf_op jit(solution)/shard_map/all_to_all | solution.py:61
  255.4 3.7 %all-to-all-start.8 = ((bf16[8,128,256]{1,2,0:T(8,128)(2,1)}), bf16[8,128,256]{1,2,0:T(8,128)(2,1)S(1)}, u32[]{:S(2)}, u32[]{:S(2)}) async-start(bf16[8,128,256]{1,2,0:T(8,128)(2,1)} %copy_bitcast_fusion.1), calls=%async_computation.8 | async-start | bytes 1048576 | tf_op jit(solution)/shard_map/all_to_all | solution.py:74
  259.1 5.5 %convolution_convert_fusion = bf16[8192,256]{1,0:T(8,128)(2,1)} fusion(bf16[8192,256]{1,0:T(8,128)(2,1)} %bitcast.3, bf16[256,256]{1,0:T(8,128)(2,1)S(1)} %bitcast.59), kind=kOutput, calls=%fused_computation | convolution fusion | flops 1075838976 | bytes 8519680 | tf_op jit(solution)/shard_map/dot_general | solution.py:78
  264.5 0.7 slice_reduce_fusion
  265.8 8.7 %all-to-all-done.8 = bf16[8,128,256]{1,2,0:T(8,128)(2,1)S(1)} async-done(((bf16[8,128,256]{1,2,0:T(8,128)(2,1)}), bf16[8,128,256]{1,2,0:T(8,128)(2,1)S(1)}, u32[]{:S(2)}, u32[]{:S(2)}) %all-to-all-start.8) | async-done | bytes 524320 | tf_op jit(solution)/shard_map/all_to_all | solution.py:74
  274.5 0.1 convert_reduce_fusion.1
  274.6 0.1 copy.52
  274.7 4.3 %fusion = bf16[8192,128]{0,1:T(8,128)(2,1)} fusion(bf16[256,8192]{1,0:T(8,128)(2,1)} %bitcast.51, f32[128,256]{1,0:T(8,128)S(1)} %get-tuple-element.30, f32[128,256]{1,0:T(8,128)S(1)} %copy.52), kind=kOutput, calls=%fused_computation.3 | convolution fusion | flops 538574848 | bytes 6553600 | tf_op jit(solution)/shard_map/dot_general | solution.py:81
  279.0 4.1 %copy.57 = bf16[8192,128]{1,0:T(8,128)(2,1)} copy(bf16[8192,128]{0,1:T(8,128)(2,1)} %fusion) | data formatting | bytes 4194304
  (14 shorter events, 0.2 us)
Async XLA Ops:
  0.6 86.8 %copy-start = (bf16[8192,128]{1,0:T(8,128)(2,1)S(1)}, bf16[8192,128]{1,0:T(8,128)(2,1)}, u32[]{:S(2)}) copy-start(bf16[8192,128]{1,0:T(8,128)(2,1)} %param.8) | copy-start | bytes 6291460
  4.4 16.8 %all-to-all-start = ((bf16[8,2,4096]{2,1,0:T(2,128)(2,1)}), bf16[8,2,4096]{2,1,0:T(2,128)(2,1)S(1)}, u32[]{:S(2)}, u32[]{:S(2)}) async-start(bf16[8,2,4096]{2,1,0:T(2,128)(2,1)} %reshape.61), calls=%async_computation | async-start | bytes 262144 | tf_op jit(solution)/shard_map/all_to_all | solution.py:13
  21.2 16.1 %all-to-all-start.5 = ((bf16[64,2,128]{2,1,0:T(2,128)(2,1)}), bf16[64,2,128]{2,1,0:T(2,128)(2,1)S(1)}, u32[]{:S(2)}, u32[]{:S(2)}) async-start(bf16[64,2,128]{2,1,0:T(2,128)(2,1)} %reshape.63), calls=%async_computation.5 | async-start | bytes 65536 | tf_op jit(solution)/shard_map/all_to_all | solution.py:31
  38.8 28.6 %all-to-all-start.1 = ((bf16[16,8,8192]{2,1,0:T(8,128)(2,1)}), bf16[16,8,8192]{2,1,0:T(8,128)(2,1)}, u32[]{:S(2)}, u32[]{:S(2)}) async-start(bf16[16,8,8192]{2,1,0:T(8,128)(2,1)} %broadcast_in_dim.43), calls=%async_computation.1 | async-start | bytes 4194304 | tf_op jit(solution)/shard_map/all_to_all | solution.py:13
  69.5 17.9 %copy-start.3 = (f32[128]{0:T(128)S(1)}, f32[128]{0:T(128)}, u32[]{:S(2)}) copy-start(f32[128]{0:T(128)} %param.9) | copy-start | bytes 1540
  81.9 10.6 %all-to-all-start.6 = ((bf16[4,64,256]{2,1,0:T(8,128)(2,1)}), bf16[4,64,256]{2,1,0:T(8,128)(2,1)S(1)}, u32[]{:S(2)}, u32[]{:S(2)}) async-start(bf16[4,64,256]{2,1,0:T(8,128)(2,1)} %stack.3), calls=%async_computation.6 | async-start | bytes 262144 | tf_op jit(solution)/shard_map/all_to_all | solution.py:35
  113.2 51.6 %all-to-all-start.4 = ((bf16[8,1024,256]{2,1,0:T(8,128)(2,1)}), bf16[8,1024,256]{2,1,0:T(8,128)(2,1)}, u32[]{:S(2)}, u32[]{:S(2)}) async-start(bf16[8,1024,256]{2,1,0:T(8,128)(2,1)} %broadcast_in_dim.48), calls=%async_computation.4 | async-start | bytes 8388608 | tf_op jit(solution)/shard_map/all_to_all | solution.py:13
  164.8 17.7 %copy-start.2 = (f32[256]{0:T(256)S(1)}, f32[256]{0:T(256)}, u32[]{:S(2)}) copy-start(f32[256]{0:T(256)} %param.11) | copy-start | bytes 3076
  164.8 17.7 %copy-start.1 = (bf16[8192,256]{1,0:T(8,128)(2,1)S(1)}, bf16[8192,256]{1,0:T(8,128)(2,1)}, u32[]{:S(2)}) copy-start(bf16[8192,256]{1,0:T(8,128)(2,1)} %param.10) | copy-start | bytes 12582916
  186.3 54.0 %all-to-all-start.7 = ((bf16[8,1024,256]{1,2,0:T(8,128)(2,1)}), bf16[8,1024,256]{1,2,0:T(8,128)(2,1)}, u32[]{:S(2)}, u32[]{:S(2)}) async-start(bf16[8,1024,256]{1,2,0:T(8,128)(2,1)} %bitcast.52), calls=%async_computation.7 | async-start | bytes 8388608 | tf_op jit(solution)/shard_map/all_to_all | solution.py:66
  241.6 13.8 %all-to-all-start.9 = ((f32[64,1,128]{2,1,0:T(1,128)}), f32[64,1,128]{2,1,0:T(1,128)S(1)}, u32[]{:S(2)}, u32[]{:S(2)}) async-start(f32[64,1,128]{2,1,0:T(1,128)} %broadcast_in_dim.49), calls=%async_computation.9 | async-start | bytes 65536 | tf_op jit(solution)/shard_map/all_to_all | solution.py:61
  255.4 19.1 %all-to-all-start.8 = ((bf16[8,128,256]{1,2,0:T(8,128)(2,1)}), bf16[8,128,256]{1,2,0:T(8,128)(2,1)S(1)}, u32[]{:S(2)}, u32[]{:S(2)}) async-start(bf16[8,128,256]{1,2,0:T(8,128)(2,1)} %copy_bitcast_fusion.1), calls=%async_computation.8 | async-start | bytes 1048576 | tf_op jit(solution)/shard_map/all_to_all | solution.py:74
